TPU v7x, 128 devices: a whole 4x4x4 slice. The times are simulated.
128 devices in a mesh: tensor: 16 (over y, x), dp: 8 (over z, core).
Axes of the slice: x: 4, y: 4, z: 4, core: 2. Of those that a mesh axis runs over, the one named last changes fastest.
Arguments:
- tokens: bfloat16 [12288, 6144], P('dp', 'tensor'), may hold values from -9 to 9
- expert_ids: int32 [12288, 2], P('dp'), may hold values from 0 to 7, as said below
- gate_probs: float32 [12288, 2], P('dp'), may hold values from 0.2 to 1
- gate_weight: bfloat16 [6144, 8192], P(None, 'tensor'), may hold values from -0.078125 to 0.078125
- up_weight: bfloat16 [6144, 8192], P(None, 'tensor'), may hold values from -0.078125 to 0.078125
- down_weight: bfloat16 [8192, 6144], P('tensor'), may hold values from -0.09375 to 0.09375
Outputs:
- expert_out: bfloat16 [12288, 6144], P('dp', 'tensor')
- peaks: float32 [2], replicated
Inputs may be any that keep to these rules, and one draw needn't show every extreme that they name: `expert_ids`: each row names two different experts. In each aligned block of 1536 rows at most 768 rows name expert 0, and in some block exactly 768 do.
All inputs are finite; a program needn't handle non-finite values.
Results may differ from a plain program's by a relative error of at most 0.02.
Values may be sent and summed in bfloat16 or wider, within the bound.
A program may use at most 128 MiB of HBM per device.

v0:
```python
import math

import jax
import jax.numpy as jnp
from jax import lax
from jax.sharding import Mesh
from jax.sharding import PartitionSpec as P

CAP = 768
TENSOR = ("tensor_0", "tensor_1")
TENSOR_DP = ("tensor_0", "tensor_1", "dp_0", "dp_1")
DP = ("dp_0", "dp_1")


clip_share = 0.25


def by_axis(x, axes):
    for axis in axes:
        x = lax.pmax(x, axis)
    return x


def sylvester(order_size):
    index_row = jnp.arange(order_size, dtype=jnp.int32)
    common = index_row[:, None] & index_row[None, :]
    parity = jnp.zeros((order_size, order_size), jnp.int32)
    for bit_pos in range(order_size.bit_length() - 1):
        parity = parity ^ common >> bit_pos & 1
    return (1 - 2 * parity).astype(jnp.float32)


def routing(expert_ids, gate_probs, capacity):
    hits = expert_ids == 0
    routed = jnp.any(hits, axis=1)
    share_of = jnp.sum(jnp.where(hits, gate_probs, 0.0), axis=1)
    position = jnp.cumsum(routed.astype(jnp.int32)) - 1
    routed_count = jnp.sum(routed.astype(jnp.int32))
    target_slot = jnp.where(routed, position, capacity)
    row_numbers = jnp.arange(expert_ids.shape[0], dtype=jnp.int32)
    source = jnp.zeros((capacity,), jnp.int32).at[target_slot].set(row_numbers, mode="drop")
    filled = jnp.arange(capacity, dtype=jnp.int32) < routed_count
    slot_of_row = jnp.clip(position, 0, capacity - 1)
    return (routed, share_of, source, filled, slot_of_row)


def rotate_rows(hidden_block):
    order_size = hidden_block.shape[1]
    bits = order_size.bit_length() - 1
    outer_size = 2 ** (bits // 2)
    inner_size = order_size // outer_size
    grid = hidden_block.astype(jnp.float32).reshape(hidden_block.shape[0], outer_size, inner_size)
    first_pass = jnp.einsum(
        "rab,bd->rad", grid, sylvester(inner_size), precision=lax.Precision.HIGHEST
    )
    second_pass = jnp.einsum(
        "rad,ac->rcd", first_pass, sylvester(outer_size), precision=lax.Precision.HIGHEST
    )
    return second_pass.reshape(hidden_block.shape[0], order_size) * (1.0 / math.sqrt(order_size))


def on_device(tokens, expert_ids, gate_probs, gate_weight, up_weight, down_weight):
    routed, share_of, source, filled, slot_of_row = routing(expert_ids, gate_probs, CAP)
    bf_zero = jnp.zeros((), tokens.dtype)
    peak_in = jnp.max(jnp.abs(jnp.where(routed[:, None], tokens, bf_zero))).astype(jnp.float32)
    picked = jnp.where(filled[:, None], tokens[source], bf_zero)
    block_in = lax.all_gather(picked, TENSOR, axis=1, tiled=True)
    gate_part = jnp.dot(block_in, gate_weight, preferred_element_type=jnp.float32)
    up_part = jnp.dot(block_in, up_weight, preferred_element_type=jnp.float32)
    hidden = (jax.nn.silu(gate_part) * up_part).astype(jnp.bfloat16)
    row_block = lax.all_to_all(hidden, TENSOR, split_axis=0, concat_axis=1, tiled=True)
    rotated = rotate_rows(row_block)
    peak_rot = jnp.max(jnp.abs(rotated))
    peak_in, peak_rot = (by_axis(peak_in, TENSOR_DP), by_axis(peak_rot, TENSOR_DP))
    clip_level = clip_share * peak_rot
    clipped = jnp.clip(rotated, -clip_level, clip_level).astype(jnp.bfloat16)
    clipped = lax.all_to_all(clipped, TENSOR, split_axis=1, concat_axis=0, tiled=True)
    partial_value = jnp.dot(clipped, down_weight, preferred_element_type=jnp.float32)
    summed = lax.psum_scatter(
        partial_value.astype(jnp.bfloat16), TENSOR, scatter_dimension=1, tiled=True
    ).astype(jnp.float32)
    expert_out = jnp.where(routed[:, None], share_of[:, None] * summed[slot_of_row], 0.0).astype(
        jnp.bfloat16
    )
    return (expert_out, jnp.stack([peak_in, peak_rot]))


def solution(mesh):
    split = Mesh(mesh.devices.reshape(4, 4, 4, 2), ("tensor_0", "tensor_1", "dp_0", "dp_1"))
    return jax.shard_map(
        on_device,
        mesh=split,
        in_specs=(
            P(DP, TENSOR),
            P(DP, None),
            P(DP, None),
            P(None, TENSOR),
            P(None, TENSOR),
            P(TENSOR, None),
        ),
        out_specs=(P(DP, TENSOR), P()),
        check_vma=False,
    )
```

profile of v0, /device:TPU:0, one launch (start us, length us, event | category | flops | bytes accessed | tf_op | source)
XLA Modules:
  0.0 319.4 jit_solution(15490799989446923589)
XLA Ops:
  7.2 0.7 fusion.70
  8.0 0.6 convert_reduce_fusion
  9.2 6.2 %scatter_custom_fusion = s32[768]{0:T(1024)S(1)} fusion(s32[1536]{0:T(1024)S(1)} %get-tuple-element.3, s32[1536]{0:T(1024)S(1)} %iota.23, s32[]{:T(128)} %constant.19.clone.1), kind=kCustom, calls=%fused_computation.93 | custom fusion | bytes 3076 | tf_op jit(solution)/shard_map/scatter | solution.py:41
  15.5 0.7 iota_compare_fusion
  16.1 3.9 %gather_fusion = bf16[768,384]{1,0:T(8,128)(2,1)S(1)} fusion(bf16[1536,384]{1,0:T(8,128)(2,1)} %param.6, s32[1024]{0:T(1024)S(1)} %pad_clamp_fusion.1), kind=kCustom, calls=%fused_computation | custom fusion | bytes 1182720 | tf_op jit(solution)/shard_map/gather | solution.py:66
  20.0 1.0 broadcast_select_fusion
  21.0 85.0 %all-gather.2.cloned.1.call-done = bf16[768,6144]{1,0:T(8,128)(2,1)} async-done(((bf16[768,384]{1,0:T(8,128)(2,1)}), bf16[768,6144]{1,0:T(8,128)(2,1)}) %all-gather.2.cloned.1.call-update) | async-done | bytes 9437200 | tf_op jit(solution)/shard_map/all_gather | solution.py:67
  106.0 9.6 %fusion.84 = f32[768,512]{1,0:T(8,128)S(1)} fusion(bf16[768,6144]{1,0:T(8,128)(2,1)} %all-gather.2.cloned.1.call-done, bf16[6144,512]{1,0:T(8,128)(2,1)} %param.9), kind=kOutput, calls=%fused_computation.110 | convolution fusion | flops 4831838208 | bytes 17301504 | tf_op jit(solution)/shard_map/dot_general | solution.py:68
  115.6 8.0 %multiply_convert_fusion = bf16[768,512]{1,0:T(8,128)(2,1)} fusion(f32[768,512]{1,0:T(8,128)S(1)} %fusion.84, bf16[768,6144]{1,0:T(8,128)(2,1)S(1)} %copy-done.3, bf16[6144,512]{1,0:T(8,128)(2,1)} %param.10), kind=kOutput, calls=%fused_computation.7 | convolution fusion | flops 4834197504 | bytes 18087936 | tf_op jit(solution)/shard_map/dot_general | solution.py:69
  123.5 5.1 %all-to-all-start = ((bf16[16,48,512]{2,1,0:T(8,128)(2,1)}), bf16[16,48,512]{2,1,0:T(8,128)(2,1)S(1)}, u32[]{:S(2)}, u32[]{:S(2)}) async-start(bf16[16,48,512]{2,1,0:T(8,128)(2,1)} %bitcast.2), calls=%async_computation | async-start | bytes 1572864 | tf_op jit(solution)/shard_map/all_to_all | solution.py:71
  128.7 1.1 abs_reduce_fusion.1
  129.7 12.0 %all-to-all-done = bf16[16,48,512]{2,1,0:T(8,128)(2,1)S(1)} async-done(((bf16[16,48,512]{2,1,0:T(8,128)(2,1)}), bf16[16,48,512]{2,1,0:T(8,128)(2,1)S(1)}, u32[]{:S(2)}, u32[]{:S(2)}) %all-to-all-start) | async-done | bytes 786464 | tf_op jit(solution)/shard_map/all_to_all | solution.py:71
  141.7 0.4 copy.10
  142.1 0.5 reshape.103
  142.6 0.8 fusion.1
  143.4 2.2 abs_reduce_fusion
  145.6 9.3 %all-reduce.2 = (f32[]{:T(128)}, f32[]{:T(128)}) all-reduce(f32[]{:T(128)} %get-tuple-element.12, bf16[]{:T(256)} %abs_reduce_fusion.1), channel_id=1, replica_groups=mesh['tensor_0'=4,'tensor_1'=4,'dp_0'=4,'dp_1'=2] {'tensor_0'}, use_global_device_ids=true, to_apply=%region_7.8 | all-reduce | flops 2 | bytes 14 | tf_op jit(solution)/shard_map/pmax | solution.py:20
  154.9 9.2 %all-reduce.1 = (f32[]{:T(128)}, f32[]{:T(128)}) all-reduce(f32[]{:T(128)} %get-tuple-element.8, f32[]{:T(128)} %get-tuple-element.9), channel_id=1, replica_groups=mesh['tensor_0'=4,'tensor_1'=4,'dp_0'=4,'dp_1'=2] {'tensor_1'}, use_global_device_ids=true, to_apply=%region_8.9 | all-reduce | flops 2 | bytes 16 | tf_op jit(solution)/shard_map/pmax | solution.py:20
  164.1 11.3 %all-reduce = (f32[]{:T(128)}, f32[]{:T(128)}) all-reduce(f32[]{:T(128)} %get-tuple-element.6, f32[]{:T(128)} %get-tuple-element.7), channel_id=1, replica_groups=mesh['tensor_0'=4,'tensor_1'=4,'dp_0'=4,'dp_1'=2] {'dp_0'}, use_global_device_ids=true, to_apply=%region_9.10 | all-reduce | flops 2 | bytes 16 | tf_op jit(solution)/shard_map/pmax | solution.py:20
  175.4 3.1 all-reduce.3
  179.2 0.5 convert_element_type.43
  179.7 0.4 copy.11
  180.1 17.7 %all_to_all.32 = bf16[48,16,512]{2,0,1:T(8,128)(2,1)S(1)} all-to-all(bf16[48,16,512]{2,0,1:T(8,128)(2,1)S(1)} %copy.11), channel_id=1, replica_groups=mesh['tensor_0'=4,'tensor_1'=4,'dp_0'=4,'dp_1'=2] {'tensor_0','tensor_1'}, dimensions={1} | all-to-all | bytes 1572864 | tf_op jit(solution)/shard_map/all_to_all | solution.py:77
  197.8 10.4 %convolution_convert_fusion = bf16[768,6144]{1,0:T(8,128)(2,1)} fusion(bf16[768,512]{1,0:T(8,128)(2,1)S(1)} %bitcast.40, bf16[512,6144]{1,0:T(8,128)(2,1)} %param.11), kind=kOutput, calls=%fused_computation.3 | convolution fusion | flops 4836556800 | bytes 16515072 | tf_op jit(solution)/shard_map/dot_general | solution.py:78
  208.3 12.7 %copy.12 = bf16[768,6144]{0,1:T(8,128)(2,1)} copy(bf16[768,6144]{1,0:T(8,128)(2,1)} %convolution_convert_fusion) | data formatting | bytes 18874368
  221.0 0.7 copy-done.1
  221.7 0.6 select_reduce_fusion
  222.3 1.8 pad_maximum_fusion
  224.2 80.3 %reduce-scatter.4.cloned.1.call-done = bf16[384,768]{1,0:T(8,128)(2,1)} async-done(((bf16[6144,768]{1,0:T(8,128)(2,1)}), bf16[384,768]{1,0:T(8,128)(2,1)}) %reduce-scatter.4.cloned.1.call-update) | async-done | bytes 589840
  304.4 1.4 copy.13
  305.9 3.7 %gather_fusion.1 = f32[1536,384]{1,0:T(8,128)S(1)} fusion(f32[768,384]{1,0:T(8,128)S(1)} %convert_element_type.45, s32[2048]{0:T(1024)S(1)} %pad_clamp_fusion), kind=kCustom, calls=%fused_computation.1 | custom fusion | bytes 4724736 | tf_op jit(solution)/shard_map/gather | solution.py:82
  309.6 2.9 select_convert_fusion
  (24 shorter events, 0.9 us)
Async XLA Ops:
  7.2 98.8 %all-gather.2.cloned.1.call-start = ((), (), s32[]{:S(2)}) async-start(), calls=%async_computation.3 | async-start | bytes 10027008 | tf_op jit(solution)/shard_map/all_gather | solution.py:67
  106.0 9.6 %copy-start.3 = (bf16[768,6144]{1,0:T(8,128)(2,1)S(1)}, bf16[768,6144]{1,0:T(8,128)(2,1)}, u32[]{:S(2)}) copy-start(bf16[768,6144]{1,0:T(8,128)(2,1)} %all-gather.2.cloned.1.call-done) | copy-start | bytes 28311556
  123.5 5.1 %copy-start = (bf16[1536,384]{1,0:T(8,128)(2,1)S(1)}, bf16[1536,384]{1,0:T(8,128)(2,1)}, u32[]{:S(2)}) copy-start(bf16[1536,384]{1,0:T(8,128)(2,1)} %param.6) | copy-start | bytes 3538948
  123.5 18.1 %all-to-all-start = ((bf16[16,48,512]{2,1,0:T(8,128)(2,1)}), bf16[16,48,512]{2,1,0:T(8,128)(2,1)S(1)}, u32[]{:S(2)}, u32[]{:S(2)}) async-start(bf16[16,48,512]{2,1,0:T(8,128)(2,1)} %bitcast.2), calls=%async_computation | async-start | bytes 1572864 | tf_op jit(solution)/shard_map/all_to_all | solution.py:71
  128.6 175.8 %reduce-scatter.4.cloned.1.call-start = ((), (), s32[]{:S(2)}) async-start(), calls=%async_computation.4 | async-start | bytes 10027008
  221.0 0.7 copy-start.1
  221.0 0.7 copy-start.2
Sparse Core Ops, SparseCore 0:
  21.1 84.8 all-gather.1
  221.1 83.2 reduce-scatter.3
where the time goes:
time: 320 us; the launch traced here: 319 us
  waiting for transfers between devices  177 us (55%)
  blocking collectives  50.6 us (16%)
  matrix products  31 us (10%)
  local copies, waits for them, and re-layouts  30.5 us (10%)
  between operations  14.8 us (5%)
  other arithmetic  10 us (3%)
  starting transfers between devices  5.16 us (2%)
    all_gather x1, waiting for transfers between devices, on_device(): block_in = lax.all_gather(picked, TENSOR, axis=1, tiled=True)  85 us
    unnamed x3, waiting for transfers between devices  80.3 us
    pmax x4, blocking collectives, by_axis(): x = lax.pmax(x, axis)  32.9 us
    all_to_all x1, blocking collectives, on_device(): lax.all_to_all(clipped, TENSOR, split_axis=1, concat_axis=0, tiled=True)  17.7 us
    unnamed x10, local copies, waits for them, and re-layouts  14.8 us
    all_to_all x1, waiting for transfers between devices, on_device(): lax.all_to_all(hidden, TENSOR, split_axis=0, concat_axis=1, tiled=True)  12 us
    dot_general x1, matrix products, on_device(): jnp.dot(clipped, down_weight, preferred_element_type=jnp.float32)  10.4 us
    dot_general x1, matrix products, on_device(): jnp.dot(block_in, gate_weight, preferred_element_type=jnp.float32)  9.56 us
  transfers between devices with their start and end apart: 3, of which 3 were waited for; matrix products, arithmetic and copies ran while one was open for 1% of the time, Pallas kernels for 0%

commit v1 on v0

v1 whole, which is shorter than its diff:
```python
import jax
import jax.numpy as jnp
from jax import lax
from jax.experimental import pallas as pl
from jax.experimental.pallas import tpu as pltpu
from jax.sharding import Mesh
from jax.sharding import PartitionSpec as P

CAP = 768
TOK = 1536
D = 6144
SL = 384
HID = 512
NCH = 3
CH = CAP // NCH
HALF = ((0, 128), (128, 128))
Y, X, Z, C = "tensor_0", "tensor_1", "dp_0", "dp_1"
TENSOR = (Y, X)
DP = (Z, C)
MESH = pl.DeviceIdType.MESH
clip_share = 0.25
BF, F32 = jnp.bfloat16, jnp.float32


def body(
    slot_row, share_row, slot_col, tok, h128, wg, wu, wd,
    out, peaks,
    xb, wgu, wd2, acc, hid, a1, rin, rout, cl, clp, s1, r1, pf, of, s2, r2, shs, pks, pkr, pkm,
    ag_r, ag_s, a1_r, a1_s, r_r, r_s, q_r, q_s, g_r, g_s, t_r, t_s,
    w1_r, w1_s, w2_r, w2_s, w3_r, w3_s, pk_r, pk_s, loc,
):
    y, x, z, c_ = (lax.axis_index(a) for a in (Y, X, Z, C))
    pos = {Y: y, X: x, Z: z, C: c_}
    size = {Y: 4, X: 4, Z: 4, C: 2}

    def nb(axis, d):
        return lax.rem(pos[axis] + (d % size[axis]), size[axis])

    def rcopy(src, dst, ss, rs, axis, d):
        return pltpu.make_async_remote_copy(
            src_ref=src, dst_ref=dst, send_sem=ss, recv_sem=rs,
            device_id={axis: nb(axis, d)}, device_id_type=MESH)

    def send(src, dst, ss, rs, axis, d):
        rcopy(src, dst, ss, rs, axis, d).start()

    def wait_r(ref, sem):
        rcopy(ref, ref, ag_s.at[0, 0], sem, X, 1).wait_recv()

    def wait_s(ref, sem):
        rcopy(ref, ref, sem, ag_r.at[0, 0, 0], X, 1).wait_send()

    def load_w():
        for n in range(2):
            pltpu.make_async_copy(wg.at[:, pl.ds(n * 256, 256)], wgu.at[n], loc.at[n]).start()
            pltpu.make_async_copy(wu.at[:, pl.ds(n * 256, 256)], wgu.at[2 + n], loc.at[2 + n]).start()

    def strip(yy, xx):
        return pl.ds(pl.multiple_of((yy * 4 + xx) * SL, 128), SL)

    def own_wd(start):
        for yy in range(4):
            k = pltpu.make_async_copy(
                wd.at[:, strip(yy, x)],
                wd2.at[yy, pl.ds(pl.multiple_of(x * HID, HID), HID), :], loc.at[4 + yy])
            k.start() if start else k.wait()

    load_w()
    own_wd(True)

    barrier = pltpu.get_barrier_semaphore()
    for axis in (Y, X, Z, C):
        for d in range(1, size[axis]):
            pl.semaphore_signal(barrier, inc=1, device_id={axis: nb(axis, d)}, device_id_type=MESH)
    pl.semaphore_wait(barrier, 10)

    me = y * 4 + x

    def pick(c):
        ids = lax.broadcasted_iota(jnp.int32, (CH, TOK), 0) + c * CH
        hit = ids == slot_row[...]
        one = jnp.where(hit, 1.0, 0.0).astype(BF)
        rows = jnp.dot(one, tok[...], preferred_element_type=F32)
        xb[me, pl.ds(c * CH, CH), :] = rows.astype(BF)
        shs[pl.ds(c * CH, CH), :] = jnp.sum(jnp.where(hit, share_row[...], 0.0), axis=1, keepdims=True)
        m = jnp.max(jnp.max(jnp.abs(rows), axis=0, keepdims=True), axis=1, keepdims=True)
        pkm[pl.ds(0, 1), :] = jnp.maximum(pkm[pl.ds(0, 1), :], m) if c else jnp.broadcast_to(m, (1, 128))

    AX = ((X, Y), (Y, X))

    def rows_of(c, h):
        o, n = HALF[h]
        return pl.ds(c * CH + o, n)

    def sid(h, ka, kb):
        a, b = AX[h]
        pa, pb = lax.rem(pos[a] + (ka % 4), 4), lax.rem(pos[b] + (kb % 4), 4)
        return pb * 4 + pa if h == 0 else pa * 4 + pb

    def piece(c, h, ka, kb):
        return xb.at[sid(h, ka, kb), rows_of(c, h)]

    def ag_send(c, h, ka, kb, which, d, idx):
        p = piece(c, h, ka, kb)
        send(p, p, ag_s.at[c, h], ag_r.at[c, h, idx], AX[h][which], d)

    def ag_wait(c, h, ka, kb, idx):
        wait_r(piece(c, h, ka, kb), ag_r.at[c, h, idx])

    def line(c, h, k):
        ag_send(c, h, k, 0, 1, 1, 3 + 3 * k)
        ag_send(c, h, k, 0, 1, -1, 4 + 3 * k)

    def ag1(c):
        for h in range(2):
            ag_send(c, h, 0, 0, 0, 1, 0)
            ag_send(c, h, 0, 0, 0, -1, 1)
        for h in range(2):
            line(c, h, 0)

    def agf1(c):
        for h in range(2):
            fwd = (c + h) % 2 == 0
            ag_wait(c, h, -1, 0, 0)
            if fwd:
                ag_send(c, h, -1, 0, 0, 1, 2)
            line(c, h, 3)
            ag_wait(c, h, 1, 0, 1)
            if not fwd:
                ag_send(c, h, 1, 0, 0, -1, 2)
            line(c, h, 1)

    def agf1b(c):
        for h in range(2):
            ag_wait(c, h, 2, 0, 2)
            line(c, h, 2)

    def agf2(c, k):
        for h in range(2):
            ag_wait(c, h, k, -1, 3 + 3 * k)
            if k % 2 == 0:
                ag_send(c, h, k, -1, 1, 1, 5 + 3 * k)
            ag_wait(c, h, k, 1, 4 + 3 * k)
            if k % 2 == 1:
                ag_send(c, h, k, 1, 1, -1, 5 + 3 * k)

    def agw(c):
        for h in range(2):
            for k in range(4):
                ag_wait(c, h, k, 2, 5 + 3 * k)

    def gu(c, sy):
        if c == 0 and sy == 0:
            for n in range(2):
                pltpu.make_async_copy(wg.at[:, pl.ds(n * 256, 256)], wgu.at[n], loc.at[n]).wait()
                pltpu.make_async_copy(wu.at[:, pl.ds(n * 256, 256)], wgu.at[2 + n], loc.at[2 + n]).wait()

        @pl.loop(0, 4)
        def _(n):
            lhs = jnp.concatenate([xb[sy * 4 + sx, pl.ds(c * CH, CH), :] for sx in range(4)], axis=1)
            r = jnp.dot(lhs, wgu[n, pl.ds(sy * 1536, 1536), :], preferred_element_type=F32)
            acc[n] = r if sy == 0 else acc[n] + r

    def act(c):
        for n in range(2):
            g = acc[n]
            hid[c, :, pl.ds(n * 256, 256)] = (g / (1.0 + jnp.exp(-g)) * acc[2 + n]).astype(BF)
        mycol = pl.ds(pl.multiple_of(x * HID, HID), HID)
        for d in (1, -1, 2):
            send(hid.at[c, pl.ds(pl.multiple_of(nb(X, d) * 64, 64), 64), :], a1.at[c, :, mycol],
                 a1_s.at[c], a1_r.at[c, d % 4 - 1], X, d)
        a1[c, :, mycol] = hid[c, pl.ds(pl.multiple_of(x * 64, 64), 64), :]

    def a2a_y(c):
        for d in (1, -1, 2):
            wait_r(a1.at[c, :, pl.ds(pl.multiple_of(nb(X, -d) * HID, HID), HID)], a1_r.at[c, d % 4 - 1])
        mycol = pl.ds(pl.multiple_of(y * 2048, 2048), 2048)
        for d in (1, -1, 2):
            send(a1.at[c, pl.ds(pl.multiple_of(nb(Y, d) * 16, 16), 16), :], rin.at[c, :, mycol],
                 r_s.at[c], r_r.at[c, d % 4 - 1], Y, d)
        rin[c, :, mycol] = a1[c, pl.ds(pl.multiple_of(y * 16, 16), 16), :]

    def rotate(c):
        for d in (1, -1, 2):
            wait_r(rin.at[c, :, pl.ds(pl.multiple_of(nb(Y, -d) * 2048, 2048), 2048)], r_r.at[c, d % 4 - 1])
        v = jnp.concatenate([rin[c, :, pl.ds(a * 128, 128)] for a in range(64)], axis=0)
        v = jnp.dot(v, h128[...], preferred_element_type=F32)
        for s in range(6):
            w = 16 << s
            v = v.reshape(1024 // (2 * w), 2, w, 128)
            p, q = v[:, 0:1], v[:, 1:2]
            v = jnp.concatenate([p + q, p - q], axis=1)
        v = v.reshape(1024, 128) * (1.0 / 8192.0 ** 0.5)
        m = jnp.max(jnp.max(jnp.abs(v), axis=0, keepdims=True), axis=1, keepdims=True)
        pkm[pl.ds(1, 1), :] = jnp.maximum(pkm[pl.ds(1, 1), :], m) if c else jnp.broadcast_to(m, (1, 128))
        v = v.astype(BF)
        for a in range(64):
            rout[c, :, pl.ds(a * 128, 128)] = v[a * 16:(a + 1) * 16]

    def back_y(c):
        myrow = pl.ds(pl.multiple_of(y * 16, 16), 16)
        for d in (1, -1, 2):
            send(rout.at[c, :, pl.ds(pl.multiple_of(nb(Y, d) * 2048, 2048), 2048)], cl.at[c, x, myrow, :],
                 q_s.at[c], q_r.at[c, d % 4 - 1], Y, d)
        cl[c, x, myrow, :] = rout[c, :, pl.ds(pl.multiple_of(y * 2048, 2048), 2048)]

    def back_x(c):
        for d in (1, -1, 2):
            wait_r(cl.at[c, x, pl.ds(pl.multiple_of(nb(Y, -d) * 16, 16), 16), :], q_r.at[c, d % 4 - 1])
        p = cl.at[c, x]
        send(p, p, g_s.at[c], g_r.at[c, 0], X, 1)
        send(p, p, g_s.at[c], g_r.at[c, 1], X, -1)

    def back_f(c):
        wait_r(cl.at[c, nb(X, -1)], g_r.at[c, 0])
        p = cl.at[c, nb(X, -1), pl.ds(0, 32), :]
        send(p, p, g_s.at[c], g_r.at[c, 2], X, 1)
        wait_r(cl.at[c, nb(X, 1)], g_r.at[c, 1])
        p = cl.at[c, nb(X, 1), pl.ds(32, 32), :]
        send(p, p, g_s.at[c], g_r.at[c, 3], X, -1)

    def back_w(c):
        wait_r(cl.at[c, nb(X, 2), pl.ds(0, 32), :], g_r.at[c, 2])
        wait_r(cl.at[c, nb(X, 2), pl.ds(32, 32), :], g_r.at[c, 3])

    e = c_ * 4 + z

    def w_1():
        src_rows = pl.ds(pl.multiple_of(e * 64, 64), 64)
        for d in (1, -1, 2):
            for yy in range(4):
                send(wd.at[src_rows, strip(yy, nb(X, d))],
                     wd2.at[yy, pl.ds(pl.multiple_of(x * HID + e * 64, 64), 64), :],
                     w1_s.at[d % 4 - 1], w1_r.at[d % 4 - 1], X, d)

    def w_rows(g, ee, n):
        return wd2.at[:, pl.ds(pl.multiple_of(g * HID + ee * 64, 64), n), :]

    def w_2():
        for d in (1, -1, 2):
            wait_r(w_rows(nb(X, -d), e, 64), w1_r.at[d % 4 - 1])
        for dz in (1, -1, 2):
            for d in (1, -1, 2):
                p = w_rows(nb(X, d), e, 64)
                send(p, p, w2_s.at[d % 4 - 1], w2_r.at[dz % 4 - 1, d % 4 - 1], Z, dz)

    def w_3():
        for dz in (1, -1, 2):
            for d in (1, -1, 2):
                wait_r(w_rows(nb(X, d), c_ * 4 + nb(Z, -dz), 64), w2_r.at[dz % 4 - 1, d % 4 - 1])
        for d in (1, -1, 2):
            p = w_rows(nb(X, d), c_ * 4, 256)
            send(p, p, w3_s.at[d % 4 - 1], w3_r.at[d % 4 - 1], C, 1)

    def w_4():
        for d in (1, -1, 2):
            wait_r(w_rows(nb(X, d), (1 - c_) * 4, 256), w3_r.at[d % 4 - 1])
        own_wd(False)

    def pk_send(i, axis):
        if i == 0:
            pks[0] = pkm[...]
        for d in range(1, size[axis]):
            send(pks.at[i], pkr.at[i, d - 1], pk_s.at[i, d - 1], pk_r.at[i, d - 1], axis, d)

    def pk_wait(i, axis):
        v = pks[i]
        for d in range(1, size[axis]):
            wait_r(pkr.at[i, d - 1], pk_r.at[i, d - 1])
            v = jnp.maximum(v, pkr[i, d - 1])
        pks[i + 1] = v

    lo, hi = pl.ds(0, 128), pl.ds(128, 128)

    def down(c):
        lim = (clip_share * pks[4, pl.ds(1, 1), pl.ds(0, 1)]).astype(BF)
        for xs in range(4):
            clp[pl.ds(xs * 64, 64), :] = jnp.minimum(jnp.maximum(cl[c, xs], -lim), lim)

        def part(d):
            return jnp.dot(clp[...], wd2[nb(Y, d)], preferred_element_type=F32)

        s1[c] = part(2).astype(BF)
        send(s1.at[c, lo, :], r1.at[c, lo, :], t_s.at[c, 0], t_r.at[c, 0], Y, -1)
        send(s1.at[c, hi, :], r1.at[c, hi, :], t_s.at[c, 0], t_r.at[c, 1], Y, 1)
        pf[c, 0] = part(-1)
        pf[c, 1] = part(1)
        of[c] = part(0)

    def down2(c):
        wait_r(r1.at[c, lo, :], t_r.at[c, 0])
        s2[c, 0, lo, :] = (pf[c, 0, lo, :] + r1[c, lo, :].astype(F32)).astype(BF)
        s2[c, 0, hi, :] = pf[c, 0, hi, :].astype(BF)
        send(s2.at[c, 0], r2.at[c, 0], t_s.at[c, 1], t_r.at[c, 2], Y, -1)
        wait_r(r1.at[c, hi, :], t_r.at[c, 1])
        s2[c, 1, lo, :] = pf[c, 1, lo, :].astype(BF)
        s2[c, 1, hi, :] = (pf[c, 1, hi, :] + r1[c, hi, :].astype(F32)).astype(BF)
        send(s2.at[c, 1], r2.at[c, 1], t_s.at[c, 1], t_r.at[c, 3], Y, 1)

    def finish(c):
        wait_r(r2.at[c, 0], t_r.at[c, 2])
        wait_r(r2.at[c, 1], t_r.at[c, 3])
        tot = of[c] + r2[c, 0].astype(F32) + r2[c, 1].astype(F32)
        sc = (tot * shs[pl.ds(c * CH, CH), :]).astype(BF)

        @pl.loop(0, TOK, step=256)
        def _(o):
            o = pl.multiple_of(o, 256)
            ids = lax.broadcasted_iota(jnp.int32, (256, CH), 1) + c * CH
            one = jnp.where(ids == slot_col[pl.ds(o, 256), :], 1.0, 0.0).astype(BF)
            r = jnp.dot(one, sc, preferred_element_type=F32).astype(BF)
            out[pl.ds(o, 256), :] = out[pl.ds(o, 256), :] + r if c else r

    pkm[...] = jnp.zeros_like(pkm)
    pick(0)
    ag1(0)
    pick(1)
    agf1(0)
    w_1()
    ag1(1)
    pick(2)
    agf1b(0)
    agf2(0, 0)
    agf2(0, 3)
    agf1(1)
    agf2(0, 1)
    agf2(0, 2)
    agf1b(1)
    ag1(2)
    agw(0)
    w_2()
    gu(0, 0)
    agf2(1, 0)
    gu(0, 1)
    agf2(1, 3)
    agf1(2)
    gu(0, 2)
    agf2(1, 1)
    gu(0, 3)
    agf2(1, 2)
    act(0)
    agf1b(2)
    agw(1)
    gu(1, 0)
    agf2(2, 0)
    gu(1, 1)
    agf2(2, 3)
    a2a_y(0)
    gu(1, 2)
    agf2(2, 1)
    gu(1, 3)
    agf2(2, 2)
    act(1)
    rotate(0)
    back_y(0)
    agw(2)
    for sy in range(4):
        gu(2, sy)
    act(2)
    a2a_y(1)
    back_x(0)
    rotate(1)
    back_y(1)
    a2a_y(2)
    back_f(0)
    rotate(2)
    pk_send(0, X)
    back_y(2)
    back_x(1)
    pk_wait(0, X)
    pk_send(1, Y)
    back_x(2)
    w_3()
    back_f(1)
    pk_wait(1, Y)
    pk_send(2, Z)
    back_w(0)
    pk_wait(2, Z)
    pk_send(3, C)
    back_f(2)
    w_4()
    pk_wait(3, C)
    peaks[...] = pks[4]
    down(0)
    back_w(1)
    down(1)
    down2(0)
    back_w(2)
    down(2)
    down2(1)
    down2(2)
    for c in range(NCH):
        finish(c)

    for c in range(NCH):
        for h in range(2):
            wait_s(xb.at[pl.ds(0, 15), rows_of(c, h)], ag_s.at[c, h])
        wait_s(hid.at[c, pl.ds(0, 192), :], a1_s.at[c])
        wait_s(a1.at[c, pl.ds(0, 48), :], r_s.at[c])
        wait_s(rout.at[c, :, pl.ds(0, 6144)], q_s.at[c])
        wait_s(cl.at[c, pl.ds(0, 3)], g_s.at[c])
        wait_s(s1.at[c], t_s.at[c, 0])
        wait_s(s2.at[c], t_s.at[c, 1])
    for d in range(3):
        wait_s(w_rows(0, 0, 64), w1_s.at[d])
        wait_s(w_rows(0, 0, 192), w2_s.at[d])
        wait_s(w_rows(0, 0, 256), w3_s.at[d])
    for i, axis in enumerate((X, Y, Z, C)):
        for d in range(1, size[axis]):
            wait_s(pks.at[i], pk_s.at[i, d - 1])


def hadamard(n):
    i = jnp.arange(n, dtype=jnp.int32)
    v = i[:, None] & i[None, :]
    p = jnp.zeros_like(v)
    for b in range(n.bit_length() - 1):
        p = p ^ (v >> b & 1)
    return (1 - 2 * p).astype(BF)


def on_device(tokens, expert_ids, gate_probs, gate_weight, up_weight, down_weight):
    hits = expert_ids == 0
    routed = jnp.any(hits, axis=1)
    share = jnp.sum(jnp.where(hits, gate_probs, 0.0), axis=1)
    slot = jnp.where(routed, jnp.cumsum(routed.astype(jnp.int32)) - 1, -1)
    vm, anyspace = pl.BlockSpec(memory_space=pltpu.VMEM), pl.BlockSpec(memory_space=pl.ANY)
    V, DMA = pltpu.VMEM, pltpu.SemaphoreType.DMA
    out, peaks = pl.pallas_call(
        body,
        name="expert",
        out_shape=(jax.ShapeDtypeStruct((TOK, SL), BF), jax.ShapeDtypeStruct((8, 128), F32)),
        in_specs=[vm] * 5 + [anyspace] * 3,
        out_specs=(vm, vm),
        scratch_shapes=[
            V((16, CAP, SL), BF),
            V((4, D, 256), BF),
            V((4, 2048, SL), BF),
            V((4, CH, 256), F32),
            V((NCH, CH, HID), BF),
            V((NCH, 64, 2048), BF),
            V((NCH, 16, 8192), BF),
            V((NCH, 16, 8192), BF),
            V((NCH, 4, 64, 2048), BF),
            V((CH, 2048), BF),
            V((NCH, CH, SL), BF),
            V((NCH, CH, SL), BF),
            V((NCH, 2, CH, SL), F32),
            V((NCH, CH, SL), F32),
            V((NCH, 2, CH, SL), BF),
            V((NCH, 2, CH, SL), BF),
            V((CAP, 1), F32),
            V((5, 8, 128), F32),
            V((4, 3, 8, 128), F32),
            V((8, 128), F32),
            DMA((NCH, 2, 15)), DMA((NCH, 2)),
            DMA((NCH, 3)), DMA((NCH,)),
            DMA((NCH, 3)), DMA((NCH,)),
            DMA((NCH, 3)), DMA((NCH,)),
            DMA((NCH, 4)), DMA((NCH,)),
            DMA((NCH, 4)), DMA((NCH, 2)),
            DMA((3,)), DMA((3,)),
            DMA((3, 3)), DMA((3,)),
            DMA((3,)), DMA((3,)),
            DMA((4, 3)), DMA((4, 3)),
            DMA((8,)),
        ],
        compiler_params=pltpu.CompilerParams(
            collective_id=0, has_side_effects=True, vmem_limit_bytes=66_000_000),
    )(slot[None, :], share[None, :], slot[:, None], tokens, hadamard(128), gate_weight, up_weight, down_weight)
    return out, peaks[:2, 0]


def solution(mesh):
    split = Mesh(mesh.devices.reshape(4, 4, 4, 2), (Y, X, Z, C))
    return jax.shard_map(
        on_device,
        mesh=split,
        in_specs=(P(DP, TENSOR), P(DP, None), P(DP, None), P(None, TENSOR), P(None, TENSOR), P(TENSOR, None)),
        out_specs=(P(DP, TENSOR), P()),
        check_vma=False,
    )
```

time: 320 us -> 146 us (0.46)
  waiting for transfers between devices: 177 us -> 0 us
  Pallas kernels: 0 us -> 135 us
  blocking collectives: 50.6 us -> 0 us
  matrix products: 31 us -> 0 us
  local copies, waits for them, and re-layouts: 30.5 us -> 4.79 us
  between operations: 14.8 us -> 0.66 us
  other arithmetic: 10 us -> 4.31 us
  starting transfers between devices: 5.16 us -> 0 us
    pallas_call x0 -> x1, Pallas kernels: none -> 135 us  [on_device(): pl.pallas_call(body, name='expert', out_shape=(jax.ShapeDtypeStruct((TOK,...]
    all_gather x1 -> x0, waiting for transfers between devices: 85 us -> none  [on_device(): block_in = lax.all_gather(picked, TENSOR, axis=1, tiled=True)]
    unnamed x3 -> x0, waiting for transfers between devices: 80.3 us -> none
    pmax x4 -> x0, blocking collectives: 32.9 us -> none  [by_axis(): x = lax.pmax(x, axis)]
    dot_general x5 -> x0, matrix products: 31 us -> none  [the longest x1 10.4 us: on_device(): jnp.dot(clipped, down_weight, preferred_element_type=jnp.float32)]
    all_to_all x1 -> x0, blocking collectives: 17.7 us -> none  [on_device(): lax.all_to_all(clipped, TENSOR, split_axis=1, concat_axis=0, tiled=True)]
    unnamed x10 -> x2, local copies, waits for them, and re-layouts: 14.8 us -> 2.69 us
    all_to_all x1 -> x0, waiting for transfers between devices: 12 us -> none  [on_device(): lax.all_to_all(hidden, TENSOR, split_axis=0, concat_axis=1, tiled=True)]
  transfers between devices with their start and end apart: 3 -> 0, of which waited for: 3 -> 0; matrix products, arithmetic and copies ran while one was open for 1% -> 0% of each run, Pallas kernels for 0% -> 0%
where the time goes in v1:
time: 146 us; the launch traced here: 145 us
  Pallas kernels  135 us (92%)
  local copies, waits for them, and re-layouts  4.79 us (3%)
  other arithmetic  4.31 us (3%)
    pallas_call x1, Pallas kernels, on_device(): pl.pallas_call(body, name='expert', out_shape=(jax.ShapeDtypeStruct((TOK,...  135 us

profile of v1, /device:TPU:0, one launch (start us, length us, event | category | flops | bytes accessed | tf_op | source)
XLA Modules:
  0.0 144.6 jit_solution(7125271419927327184)
XLA Ops:
  0.6 0.7 fusion
  1.4 0.3 reduce-window.9
  1.7 0.1 slice.13
  1.8 0.1 slice_reduce_fusion
  1.9 0.1 add_bitcast_fusion
  2.0 0.6 reshape_select_fusion
  2.6 0.7 select_reduce_fusion
  3.3 0.6 broadcast_in_dim.14.share_row
  3.9 0.7 subtract_convert_fusion.h128
  4.6 0.3 copy.12
  4.9 1.2 bitcast_select_fusion.slot_col
  6.0 134.9 %expert.1 = (bf16[1536,384]{1,0:T(8,128)(2,1)}, f32[8,128]{1,0:T(8,128)}) custom-call(s32[1,1536]{1,0:T(1,128)} %get-tuple-element.6.slot_row, f32[1,1536]{1,0:T(1,128)} %broadcast_in_dim.14.share_row, s32[1536,1]{1,0:T(8,128)} %bitcast_select_fusion.slot_col, bf16[1536,384]{1,0:T(8,128)(2,1)} %tok.1, bf16[128,128]{1,0:T(8,128)(2,1)} %subtract_convert_fusion.h128, ...), custom_call_target="tpu_custom_call" | custom-call | tf_op jit(solution)/shard_map/expert/pallas_call | solution.py:429
  140.9 1.3 slice_reduce_fusion.1
  142.2 2.4 %copy.16 = bf16[1536,384]{1,0:T(8,128)(2,1)} copy(bf16[1536,384]{1,0:T(8,128)(2,1)} %get-tuple-element.10) | data formatting | bytes 2359296
  (2 shorter events, 0.0 us)

commit v2 on v0

v2 whole, which is shorter than its diff:
```python
import jax
import jax.numpy as jnp
from jax import lax
from jax.experimental import pallas as pl
from jax.experimental.pallas import tpu as pltpu
from jax.sharding import Mesh
from jax.sharding import PartitionSpec as P

CAP = 768
TOK = 1536
D = 6144
SL = 384
HID = 512
NCH = 3
CH = CAP // NCH
Y, X, Z, C = "tensor_0", "tensor_1", "dp_0", "dp_1"
TENSOR = (Y, X)
DP = (Z, C)
MESH = pl.DeviceIdType.MESH
clip_share = 0.25
BF, F32 = jnp.bfloat16, jnp.float32
PLANE = [(du, dv) for du in (1, -1, 2, 0) for dv in (1, -1, 2, 0) if du or dv]
DEPTH = [(dz, dc) for dz in (0, 1, -1, 2) for dc in (0, 1) if dz or dc]


def body(
    slot_row, share_row, slot_col, tok, h128, wg, wu, wd,
    out, peaks,
    xb, wgu, wd2, acc, hid, rin, rout, cl, clp, s1, r1, pf, of, s2, r2, shs, pks, pkr, pkm,
    ag_r, ag_s, a_r, a_s, q_r, q_s, g_r, g_s, t_r, t_s, w1_r, w1_s, w2_r, w2_s, pk_r, pk_s, loc,
):
    y, x, z, c_ = (lax.axis_index(a) for a in (Y, X, Z, C))
    n_ = 1 - c_
    u, v = x * n_ + y * c_, y * n_ + x * c_

    def pu(d):
        return lax.rem(u + (d + 4), 4)

    def pv(d):
        return lax.rem(v + (d + 4), 4)

    def at_uv(du, dv):
        return {Y: lax.rem(y + (du * c_ + dv * n_) + 4, 4), X: lax.rem(x + (du * n_ + dv * c_) + 4, 4)}

    def at_zc(dz, dc):
        return {Z: lax.rem(z + (dz + 4), 4), C: lax.rem(c_ + dc, 2)}

    def rcopy(src, dst, ss, rs, to):
        return pltpu.make_async_remote_copy(
            src_ref=src, dst_ref=dst, send_sem=ss, recv_sem=rs, device_id=to, device_id_type=MESH)

    def send(src, dst, ss, rs, to):
        rcopy(src, dst, ss, rs, to).start()

    def wait_s(ref, sem):
        rcopy(ref, ref, sem, pk_r.at[0], at_uv(1, 0)).wait_send()

    seen = set()

    def need(key, ref, sem):
        if key not in seen:
            seen.add(key)
            rcopy(ref, ref, pk_s.at[0], sem, at_uv(1, 0)).wait_recv()

    def mul(i, n):
        return pl.ds(pl.multiple_of(i * n, n), n)

    def tid(uu, vv):
        return (vv * 4 + uu) * n_ + (uu * 4 + vv) * c_

    def own_wd(start):
        for vv in range(4):
            k = pltpu.make_async_copy(wd.at[:, mul(tid(u, vv), SL)], wd2.at[vv, mul(u, HID), :], loc.at[4 + vv])
            k.start() if start else k.wait()

    def load():
        @pl.loop(0, 16)
        def _(s):
            src, dst = mul(tid(lax.rem(s, 4), s // 4), SL), mul(s, SL)
            for n in range(2):
                pltpu.make_async_copy(wg.at[src, pl.ds(n * 256, 256)], wgu.at[n, dst, :], loc.at[n]).start()
                pltpu.make_async_copy(wu.at[src, pl.ds(n * 256, 256)], wgu.at[2 + n, dst, :], loc.at[2 + n]).start()

        own_wd(True)

    me = v * 4 + u

    def pick(c):
        ids = lax.broadcasted_iota(jnp.int32, (CH, TOK), 0) + c * CH
        hit = ids == slot_row[...]
        one = jnp.where(hit, 1.0, 0.0).astype(BF)
        rows = jnp.dot(one, tok[...], preferred_element_type=F32)
        xb[me, pl.ds(c * CH, CH), :] = rows.astype(BF)
        shs[pl.ds(c * CH, CH), :] = jnp.sum(jnp.where(hit, share_row[...], 0.0), axis=1, keepdims=True)
        m = jnp.max(jnp.max(jnp.abs(rows), axis=0, keepdims=True), axis=1, keepdims=True)
        pkm[pl.ds(0, 1), :] = jnp.maximum(pkm[pl.ds(0, 1), :], m)

    def rows_of(c, h):
        return pl.ds(c * CH + h * 128, 128)

    def piece(c, h, ka, kb):
        du, dv = (ka, kb) if h == 0 else (kb, ka)
        return xb.at[pv(dv) * 4 + pu(du), rows_of(c, h)]

    def ag_send(c, h, ka, kb, second, d, idx):
        p = piece(c, h, ka, kb)
        along_u = (h == 0) != second
        send(p, p, ag_s.at[c, h], ag_r.at[c, h, idx], at_uv(d, 0) if along_u else at_uv(0, d))

    def ag_need(c, h, idx):
        if idx < 3:
            ka, kb = (-1, 1, 2)[idx], 0
        else:
            ka, kb = (idx - 3) // 3, (-1, 1, 2)[(idx - 3) % 3]
        need(("ag", c, h, idx), piece(c, h, ka, kb), ag_r.at[c, h, idx])

    def line(c, h, k):
        ag_send(c, h, k, 0, True, 1, 3 + 3 * k)
        ag_send(c, h, k, 0, True, -1, 4 + 3 * k)

    def own(c, h):
        ag_send(c, h, 0, 0, False, 1, 0)
        ag_send(c, h, 0, 0, False, -1, 1)
        line(c, h, 0)

    def r(c, h, k):
        forward = (c + h) % 2 == 0
        ag_need(c, h, {3: 0, 1: 1, 2: 2}[k])
        if k == 3 and forward:
            ag_send(c, h, -1, 0, False, 1, 2)
        if k == 1 and not forward:
            ag_send(c, h, 1, 0, False, -1, 2)
        line(c, h, k)

    def f(c, h, k):
        if k % 2 == 0:
            ag_need(c, h, 3 + 3 * k)
            ag_send(c, h, k, -1, True, 1, 5 + 3 * k)
        else:
            ag_need(c, h, 4 + 3 * k)
            ag_send(c, h, k, 1, True, -1, 5 + 3 * k)

    started = set()

    def gu(c, dv):
        if dv == 0:
            idxs = [(0, i) for i in (0, 1, 2)] + [(1, i) for i in (3, 4, 5)]
        else:
            e = {1: 1, 3: 0, 2: 2}[dv]
            idxs = [(0, 3 + 3 * k + e) for k in range(4)] + [(1, e)] + [(1, 3 + 3 * dv + i) for i in range(3)]
        for h, i in idxs:
            ag_need(c, h, i)
        if not started:
            for n in range(4):
                pltpu.make_async_copy(wg.at[:, pl.ds(0, 256)], wgu.at[n], loc.at[n]).wait()
        first = c not in started
        started.add(c)
        vv = pv(dv)

        @pl.loop(0, 4)
        def _(n):
            lhs = jnp.concatenate([xb[vv * 4 + uu, pl.ds(c * CH, CH), :] for uu in range(4)], axis=1)
            t = jnp.dot(lhs, wgu[n, mul(vv, 1536), :], preferred_element_type=F32)
            acc[c, n] = t if first else acc[c, n] + t

    def act(c):
        for n in range(2):
            g = acc[c, n]
            hid[c, :, pl.ds(n * 256, 256)] = (g / (1.0 + jnp.exp(-g)) * acc[c, 2 + n]).astype(BF)
        for du, dv in PLANE:
            send(hid.at[c, mul(pu(du) * 4 + pv(dv), 16), :], rin.at[c, :, mul(me, HID)],
                 a_s.at[c], a_r.at[c], at_uv(du, dv))
        rin[c, :, mul(me, HID)] = hid[c, mul(u * 4 + v, 16), :]

    def rot(c):
        need(("a", c), rin.at[c, :, pl.ds(0, 15 * HID)], a_r.at[c])
        w = jnp.concatenate([rin[c, :, pl.ds(a * 128, 128)] for a in range(64)], axis=0)
        w = jnp.dot(w, h128[...], preferred_element_type=F32)
        for s in range(6):
            n = 16 << s
            w = w.reshape(1024 // (2 * n), 2, n, 128)
            p, q = w[:, 0:1], w[:, 1:2]
            w = jnp.concatenate([p + q, p - q], axis=1)
        w = w.reshape(1024, 128) * (1.0 / 8192.0 ** 0.5)
        m = jnp.max(jnp.max(jnp.abs(w), axis=0, keepdims=True), axis=1, keepdims=True)
        pkm[pl.ds(1, 1), :] = jnp.maximum(pkm[pl.ds(1, 1), :], m)
        w = w.astype(BF)
        for a in range(64):
            rout[c, :, pl.ds(a * 128, 128)] = w[a * 16:(a + 1) * 16]

    def by(c):
        for d in (1, -1, 2):
            send(rout.at[c, :, mul(pv(d), 2048)], cl.at[c, u, mul(v, 16), :],
                 q_s.at[c], q_r.at[c, d % 4 - 1], at_uv(0, d))
        cl[c, u, mul(v, 16), :] = rout[c, :, mul(v, 2048)]

    lo32, hi32 = pl.ds(0, 32), pl.ds(32, 32)

    def by_need(c):
        for d in (1, -1, 2):
            need(("q", c, d), cl.at[c, u, mul(pv(-d), 16), :], q_r.at[c, d % 4 - 1])

    def bx(c):
        by_need(c)
        for part, d, i in ((lo32, 1, 0), (hi32, -1, 3), (hi32, 1, 1), (lo32, -1, 2)):
            p = cl.at[c, u, part, :]
            send(p, p, g_s.at[c], g_r.at[c, i], at_uv(d, 0))

    def bf(c, d):
        if d == -1:
            p = cl.at[c, pu(-1), lo32, :]
            need(("g", c, 0), p, g_r.at[c, 0])
            send(p, p, g_s.at[c], g_r.at[c, 4], at_uv(1, 0))
        else:
            p = cl.at[c, pu(1), hi32, :]
            need(("g", c, 3), p, g_r.at[c, 3])
            send(p, p, g_s.at[c], g_r.at[c, 5], at_uv(-1, 0))

    def clip(c):
        by_need(c)
        for i, (k, part) in enumerate(((-1, lo32), (-1, hi32), (1, lo32), (1, hi32), (2, lo32), (2, hi32))):
            need(("g", c, i), cl.at[c, pu(k), part, :], g_r.at[c, i])
        lim = (clip_share * pks[2, pl.ds(1, 1), pl.ds(0, 1)]).astype(BF)
        for uu in range(4):
            clp[c, pl.ds(uu * 64, 64), :] = jnp.minimum(jnp.maximum(cl[c, uu], -lim), lim)

    def w_rows(g, zz):
        return wd2.at[:, pl.ds(pl.multiple_of(g * HID + zz * 128, 128), 128), :]

    def w1():
        for d in (1, -1, 2):
            for vv in range(4):
                send(wd.at[mul(z, 128), mul(tid(pu(d), vv), SL)],
                     wd2.at[vv, pl.ds(pl.multiple_of(u * HID + z * 128, 128), 128), :],
                     w1_s.at[d % 4 - 1], w1_r.at[d % 4 - 1], at_uv(d, 0))

    def w2():
        for d in (1, -1, 2):
            need(("w1", d), w_rows(pu(-d), z), w1_r.at[d % 4 - 1])
        for dz in (1, -1, 2):
            for d in (1, -1, 2):
                p = w_rows(pu(d), z)
                send(p, p, w2_s.at[d % 4 - 1], w2_r.at[dz % 4 - 1, d % 4 - 1], at_zc(dz, 0))

    STAGES = ((DEPTH, at_zc), (PLANE, at_uv))

    def pks_(i):
        if i == 0:
            pks[0] = pkm[...]
        for j, to in enumerate(STAGES[i][0]):
            send(pks.at[i], pkr.at[i, j], pk_s.at[i], pk_r.at[i], STAGES[i][1](*to))

    def pkw(i):
        n = len(STAGES[i][0])
        need(("pk", i), pkr.at[i, pl.ds(0, n)], pk_r.at[i])
        pks[i + 1] = jnp.maximum(pks[i], jnp.max(pkr[i, pl.ds(0, n)], axis=0))
        if i == 1:
            peaks[...] = pks[2]

    lo, hi = pl.ds(0, 128), pl.ds(128, 128)

    def d(c, k):
        for dz in (1, -1, 2):
            for j in (1, -1, 2):
                need(("w2", dz, j), w_rows(pu(j), lax.rem(z - dz + 4, 4)), w2_r.at[dz % 4 - 1, j % 4 - 1])
        if "wd" not in seen:
            seen.add("wd")
            own_wd(False)
        t = jnp.dot(clp[c], wd2[pv(k)], preferred_element_type=F32)
        if k == 2:
            s1[c] = t.astype(BF)
            send(s1.at[c, lo, :], r1.at[c, lo, :], t_s.at[c, 0], t_r.at[c, 0], at_uv(0, -1))
            send(s1.at[c, hi, :], r1.at[c, hi, :], t_s.at[c, 0], t_r.at[c, 1], at_uv(0, 1))
        elif k == 0:
            of[c] = t
        else:
            pf[c, (k + 1) // 2] = t

    def s(c, k):
        if k == -1:
            need(("t", c, 0), r1.at[c, lo, :], t_r.at[c, 0])
            s2[c, 0, lo, :] = (pf[c, 0, lo, :] + r1[c, lo, :].astype(F32)).astype(BF)
            s2[c, 0, hi, :] = pf[c, 0, hi, :].astype(BF)
            send(s2.at[c, 0], r2.at[c, 0], t_s.at[c, 1], t_r.at[c, 2], at_uv(0, -1))
        else:
            need(("t", c, 1), r1.at[c, hi, :], t_r.at[c, 1])
            s2[c, 1, lo, :] = pf[c, 1, lo, :].astype(BF)
            s2[c, 1, hi, :] = (pf[c, 1, hi, :] + r1[c, hi, :].astype(F32)).astype(BF)
            send(s2.at[c, 1], r2.at[c, 1], t_s.at[c, 1], t_r.at[c, 3], at_uv(0, 1))

    done = set()

    def fin(c):
        need(("t", c, 2), r2.at[c, 0], t_r.at[c, 2])
        need(("t", c, 3), r2.at[c, 1], t_r.at[c, 3])
        tot = of[c] + r2[c, 0].astype(F32) + r2[c, 1].astype(F32)
        sc = (tot * shs[pl.ds(c * CH, CH), :]).astype(BF)
        first = not done
        done.add(c)

        @pl.loop(0, TOK, step=256)
        def _(o):
            o = pl.multiple_of(o, 256)
            ids = lax.broadcasted_iota(jnp.int32, (256, CH), 1) + c * CH
            one = jnp.where(ids == slot_col[pl.ds(o, 256), :], 1.0, 0.0).astype(BF)
            t = jnp.dot(one, sc, preferred_element_type=F32).astype(BF)
            out[pl.ds(o, 256), :] = t if first else out[pl.ds(o, 256), :] + t

    barrier = pltpu.get_barrier_semaphore()
    for i, to in STAGES:
        for t in i:
            pl.semaphore_signal(barrier, inc=1, device_id=to(*t), device_id_type=MESH)
    pl.semaphore_wait(barrier, len(PLANE) + len(DEPTH))
    pkm[...] = jnp.zeros_like(pkm)

    steps = (
        (pick, 0), (own, 0, 1), (pick, 2), (own, 0, 0), (load,), (pick, 1), (w1,), (r, 0, 1, 1), (f, 0, 1, 0),
        (r, 0, 1, 3), (r, 0, 0, 3), (f, 0, 0, 0), (r, 0, 0, 1), (own, 1, 0), (r, 0, 1, 2), (f, 0, 0, 1),
        (f, 1, 0, 0), (w2,), (f, 0, 1, 1), (f, 0, 1, 3), (r, 1, 0, 1), (r, 0, 0, 2), (own, 1, 1), (gu, 0, 0),
        (r, 1, 0, 3), (f, 1, 0, 1), (f, 0, 1, 2), (gu, 0, 3), (r, 1, 0, 2), (f, 1, 1, 0), (f, 0, 0, 2),
        (gu, 0, 1), (r, 1, 1, 1), (own, 2, 0), (own, 2, 1), (f, 0, 0, 3), (f, 1, 0, 3), (gu, 1, 0),
        (r, 1, 1, 3), (f, 1, 1, 1), (f, 1, 0, 2), (r, 2, 0, 1), (r, 2, 0, 3), (r, 2, 1, 1), (f, 2, 1, 0),
        (r, 2, 1, 3), (f, 1, 1, 3), (gu, 0, 2), (act, 0), (gu, 1, 1), (r, 2, 0, 2), (f, 2, 1, 1),
        (f, 2, 0, 1), (r, 1, 1, 2), (f, 2, 1, 3), (f, 2, 0, 3), (gu, 2, 0), (gu, 1, 3), (r, 2, 1, 2),
        (f, 2, 0, 2), (f, 1, 1, 2), (gu, 2, 1), (f, 2, 1, 2), (rot, 0), (f, 2, 0, 0), (by, 0), (gu, 1, 2),
        (act, 1), (gu, 2, 3), (gu, 2, 2), (act, 2), (bx, 0), (rot, 1), (by, 1), (bf, 0, 1), (bf, 0, -1),
        (rot, 2), (pks_, 0), (by, 2), (bx, 1), (pkw, 0), (pks_, 1), (bx, 2), (bf, 1, 1), (bf, 1, -1),
        (bf, 2, 1), (bf, 2, -1), (pkw, 1), (clip, 0), (d, 0, 2), (d, 0, -1), (d, 0, 0), (clip, 1), (d, 1, 2),
        (d, 1, 0), (d, 1, 1), (d, 1, -1), (clip, 2), (d, 2, 2), (d, 2, 1), (s, 1, 1), (s, 1, -1), (d, 2, 0),
        (d, 0, 1), (s, 0, 1), (s, 0, -1), (d, 2, -1), (s, 2, 1), (s, 2, -1), (fin, 1), (fin, 0), (fin, 2),
    )
    for step, *args in steps:
        step(*args)

    for c in range(NCH):
        for h in range(2):
            wait_s(xb.at[pl.ds(0, 15), rows_of(c, h)], ag_s.at[c, h])
        wait_s(hid.at[c, pl.ds(0, 240), :], a_s.at[c])
        wait_s(rout.at[c, :, pl.ds(0, 6144)], q_s.at[c])
        wait_s(cl.at[c, pl.ds(0, 3)], g_s.at[c])
        wait_s(s1.at[c], t_s.at[c, 0])
        wait_s(s2.at[c], t_s.at[c, 1])
    for i in range(3):
        wait_s(w_rows(0, 0), w1_s.at[i])
        wait_s(wd2.at[:, pl.ds(0, 384), :], w2_s.at[i])
    for i in range(2):
        wait_s(pkr.at[i, pl.ds(0, len(STAGES[i][0]))], pk_s.at[i])


def hadamard(n):
    i = jnp.arange(n, dtype=jnp.int32)
    v = i[:, None] & i[None, :]
    p = jnp.zeros_like(v)
    for b in range(n.bit_length() - 1):
        p = p ^ (v >> b & 1)
    return (1 - 2 * p).astype(BF)


def on_device(tokens, expert_ids, gate_probs, gate_weight, up_weight, down_weight):
    hits = expert_ids == 0
    routed = jnp.any(hits, axis=1)
    share = jnp.sum(jnp.where(hits, gate_probs, 0.0), axis=1)
    slot = jnp.where(routed, jnp.cumsum(routed.astype(jnp.int32)) - 1, -1)
    vm, anyspace = pl.BlockSpec(memory_space=pltpu.VMEM), pl.BlockSpec(memory_space=pl.ANY)
    V, DMA = pltpu.VMEM, pltpu.SemaphoreType.DMA
    out, peaks = pl.pallas_call(
        body,
        name="expert",
        out_shape=(jax.ShapeDtypeStruct((TOK, SL), BF), jax.ShapeDtypeStruct((8, 128), F32)),
        in_specs=[vm] * 5 + [anyspace] * 3,
        out_specs=(vm, vm),
        scratch_shapes=[
            V((16, CAP, SL), BF),
            V((4, D, 256), BF),
            V((4, 2048, SL), BF),
            V((NCH, 4, CH, 256), F32),
            V((NCH, CH, HID), BF),
            V((NCH, 16, 8192), BF),
            V((NCH, 16, 8192), BF),
            V((NCH, 4, 64, 2048), BF),
            V((NCH, CH, 2048), BF),
            V((NCH, CH, SL), BF),
            V((NCH, CH, SL), BF),
            V((NCH, 2, CH, SL), F32),
            V((NCH, CH, SL), F32),
            V((NCH, 2, CH, SL), BF),
            V((NCH, 2, CH, SL), BF),
            V((CAP, 1), F32),
            V((3, 8, 128), F32),
            V((2, 15, 8, 128), F32),
            V((8, 128), F32),
            DMA((NCH, 2, 15)), DMA((NCH, 2)),
            DMA((NCH,)), DMA((NCH,)),
            DMA((NCH, 3)), DMA((NCH,)),
            DMA((NCH, 6)), DMA((NCH,)),
            DMA((NCH, 4)), DMA((NCH, 2)),
            DMA((3,)), DMA((3,)),
            DMA((3, 3)), DMA((3,)),
            DMA((2,)), DMA((2,)),
            DMA((8,)),
        ],
        compiler_params=pltpu.CompilerParams(
            collective_id=0, has_side_effects=True, vmem_limit_bytes=66_000_000),
    )(slot[None, :], share[None, :], slot[:, None], tokens, hadamard(128), gate_weight, up_weight, down_weight)
    return out, peaks[:2, 0]


def solution(mesh):
    split = Mesh(mesh.devices.reshape(4, 4, 4, 2), (Y, X, Z, C))
    return jax.shard_map(
        on_device,
        mesh=split,
        in_specs=(P(DP, TENSOR), P(DP, None), P(DP, None), P(None, TENSOR), P(None, TENSOR), P(TENSOR, None)),
        out_specs=(P(DP, TENSOR), P()),
        check_vma=False,
    )
```

time: 320 us -> 126 us (0.39)
  waiting for transfers between devices: 177 us -> 0 us
  Pallas kernels: 0 us -> 116 us
  blocking collectives: 50.6 us -> 0 us
  matrix products: 31 us -> 0 us
  local copies, waits for them, and re-layouts: 30.5 us -> 4.79 us
  between operations: 14.8 us -> 0.66 us
  other arithmetic: 10 us -> 4.31 us
  starting transfers between devices: 5.16 us -> 0 us
    pallas_call x0 -> x1, Pallas kernels: none -> 116 us  [on_device(): pl.pallas_call(body, name='expert', out_shape=(jax.ShapeDtypeStruct((TOK,...]
    all_gather x1 -> x0, waiting for transfers between devices: 85 us -> none  [on_device(): block_in = lax.all_gather(picked, TENSOR, axis=1, tiled=True)]
    unnamed x3 -> x0, waiting for transfers between devices: 80.3 us -> none
    pmax x4 -> x0, blocking collectives: 32.9 us -> none  [by_axis(): x = lax.pmax(x, axis)]
    dot_general x5 -> x0, matrix products: 31 us -> none  [the longest x1 10.4 us: on_device(): jnp.dot(clipped, down_weight, preferred_element_type=jnp.float32)]
    all_to_all x1 -> x0, blocking collectives: 17.7 us -> none  [on_device(): lax.all_to_all(clipped, TENSOR, split_axis=1, concat_axis=0, tiled=True)]
    unnamed x10 -> x2, local copies, waits for them, and re-layouts: 14.8 us -> 2.69 us
    all_to_all x1 -> x0, waiting for transfers between devices: 12 us -> none  [on_device(): lax.all_to_all(hidden, TENSOR, split_axis=0, concat_axis=1, tiled=True)]
  transfers between devices with their start and end apart: 3 -> 0, of which waited for: 3 -> 0; matrix products, arithmetic and copies ran while one was open for 1% -> 0% of each run, Pallas kernels for 0% -> 0%
where the time goes in v2:
time: 126 us
  Pallas kernels  116 us (92%)
  local copies, waits for them, and re-layouts  4.79 us (4%)
  other arithmetic  4.31 us (3%)
    pallas_call x1, Pallas kernels, on_device(): pl.pallas_call(body, name='expert', out_shape=(jax.ShapeDtypeStruct((TOK,...  116 us
    unnamed x2, local copies, waits for them, and re-layouts  2.69 us

profile of v2, /device:TPU:0, one launch (start us, length us, event | category | flops | bytes accessed | tf_op | source)
XLA Modules:
  0.0 125.8 jit_solution(330080686398065535)
XLA Ops:
  0.6 0.7 fusion
  1.4 0.3 reduce-window.9
  1.7 0.1 slice.13
  1.8 0.1 slice_reduce_fusion
  1.9 0.1 add_bitcast_fusion
  2.0 0.6 reshape_select_fusion
  2.6 0.7 select_reduce_fusion
  3.3 0.6 broadcast_in_dim.14.share_row
  3.9 0.7 subtract_convert_fusion.h128
  4.6 0.3 copy.12
  4.9 1.2 bitcast_select_fusion.slot_col
  6.0 116.1 %expert.1 = (bf16[1536,384]{1,0:T(8,128)(2,1)}, f32[8,128]{1,0:T(8,128)}) custom-call(s32[1,1536]{1,0:T(1,128)} %get-tuple-element.6.slot_row, f32[1,1536]{1,0:T(1,128)} %broadcast_in_dim.14.share_row, s32[1536,1]{1,0:T(8,128)} %bitcast_select_fusion.slot_col, bf16[1536,384]{1,0:T(8,128)(2,1)} %tok.1, bf16[128,128]{1,0:T(8,128)(2,1)} %subtract_convert_fusion.h128, ...), custom_call_target="tpu_custom_call" | custom-call | tf_op jit(solution)/shard_map/expert/pallas_call | solution.py:366
  122.1 1.3 %slice_reduce_fusion.1 = f32[2]{0:T(128)} fusion(f32[8,128]{1,0:T(8,128)} %get-tuple-element.5), kind=kLoop, calls=%fused_computation.9 | loop fusion | bytes 16 | tf_op jit(solution)/shard_map/slice | solution.py:405
  123.4 2.4 %copy.16 = bf16[1536,384]{1,0:T(8,128)(2,1)} copy(bf16[1536,384]{1,0:T(8,128)(2,1)} %get-tuple-element.10) | data formatting | bytes 2359296
  (2 shorter events, 0.0 us)

commit v3 on v2

--- a/solution.py
+++ b/solution.py
@@ -24,9 +24,9 @@
 
 
 def body(
-    slot_row, share_row, slot_col, tok, h128, wg, wu, wd,
-    out, peaks,
-    xb, wgu, wd2, acc, hid, rin, rout, cl, clp, s1, r1, pf, of, s2, r2, shs, pks, pkr, pkm,
+    ids, probs, tok_hbm, wg, wu, wd,
+    out_hbm, peaks,
+    xb, wgu, wd2, acc, hid, rin, rout, cl, clp, s1, r1, pf, of, s2, r2, shs, pks, pkr, pkm, srow, scol, ex_m, tok, out, h128,
     ag_r, ag_s, a_r, a_s, q_r, q_s, g_r, g_s, t_r, t_s, w1_r, w1_s, w2_r, w2_s, pk_r, pk_s, loc,
 ):
     y, x, z, c_ = (lax.axis_index(a) for a in (Y, X, Z, C))
@@ -83,15 +83,40 @@
 
         own_wd(True)
 
+    tok_copy = pltpu.make_async_copy(tok_hbm, tok, loc.at[8])
+    tok_copy.start()
+
     me = v * 4 + u
 
+    def head():
+        i, j = (lax.broadcasted_iota(jnp.int32, (128, 128), a) for a in (0, 1))
+        both, sign = i & j, jnp.zeros((128, 128), jnp.int32)
+        for b in range(7):
+            sign = sign ^ (both >> b & 1)
+        h128[...] = (1 - 2 * sign).astype(F32).astype(BF)
+        e0, e1 = ids[pl.ds(0, 1), :] == 0, ids[pl.ds(1, 1), :] == 0
+        on = jnp.where(e0 | e1, 1.0, 0.0)
+        srow[pl.ds(1, 1), :] = (
+            jnp.where(e0, probs[pl.ds(0, 1), :], 0.0) + jnp.where(e1, probs[pl.ds(1, 1), :], 0.0))
+        on = jnp.concatenate(
+            [on[:, a * 128:(a + 1) * 128] for a in range(12)] + [jnp.zeros((4, 128), F32)], axis=0)
+        i, j = (lax.broadcasted_iota(jnp.int32, (128, 128), a) for a in (0, 1))
+        cum = jnp.dot(on.astype(BF), jnp.where(i <= j, 1.0, 0.0).astype(BF), preferred_element_type=F32)
+        tot = jnp.broadcast_to(cum[:, 127:128], (16, 128)).astype(BF)
+        i, j = (lax.broadcasted_iota(jnp.int32, (16, 16), a) for a in (0, 1))
+        off = jnp.dot(jnp.where(i > j, 1.0, 0.0).astype(BF), tot, preferred_element_type=F32)
+        slot = jnp.where(on > 0.5, cum + off - 1.0, -1.0)
+        srow[pl.ds(0, 1), :] = jnp.concatenate([slot[a:a + 1, :] for a in range(12)], axis=1)
+        scol[...] = jnp.concatenate([slot, jnp.zeros((112, 128), F32)], axis=0).T
+
     def pick(c):
-        ids = lax.broadcasted_iota(jnp.int32, (CH, TOK), 0) + c * CH
-        hit = ids == slot_row[...]
+        hit = (lax.broadcasted_iota(jnp.int32, (CH, TOK), 0) + c * CH).astype(F32) == srow[pl.ds(0, 1), :]
         one = jnp.where(hit, 1.0, 0.0).astype(BF)
+        if c == 0:
+            tok_copy.wait()
         rows = jnp.dot(one, tok[...], preferred_element_type=F32)
         xb[me, pl.ds(c * CH, CH), :] = rows.astype(BF)
-        shs[pl.ds(c * CH, CH), :] = jnp.sum(jnp.where(hit, share_row[...], 0.0), axis=1, keepdims=True)
+        shs[pl.ds(c * CH, CH), :] = jnp.sum(jnp.where(hit, srow[pl.ds(1, 1), :], 0.0), axis=1, keepdims=True)
         m = jnp.max(jnp.max(jnp.abs(rows), axis=0, keepdims=True), axis=1, keepdims=True)
         pkm[pl.ds(0, 1), :] = jnp.maximum(pkm[pl.ds(0, 1), :], m)
 
@@ -255,7 +280,8 @@
         need(("pk", i), pkr.at[i, pl.ds(0, n)], pk_r.at[i])
         pks[i + 1] = jnp.maximum(pks[i], jnp.max(pkr[i, pl.ds(0, n)], axis=0))
         if i == 1:
-            peaks[...] = pks[2]
+            peaks[0] = pks[2, 0, 0]
+            peaks[1] = pks[2, 1, 0]
 
     lo, hi = pl.ds(0, 128), pl.ds(128, 128)
 
@@ -297,14 +323,23 @@
         sc = (tot * shs[pl.ds(c * CH, CH), :]).astype(BF)
         first = not done
         done.add(c)
+        last = len(done) == NCH
 
         @pl.loop(0, TOK, step=256)
         def _(o):
             o = pl.multiple_of(o, 256)
-            ids = lax.broadcasted_iota(jnp.int32, (256, CH), 1) + c * CH
-            one = jnp.where(ids == slot_col[pl.ds(o, 256), :], 1.0, 0.0).astype(BF)
-            t = jnp.dot(one, sc, preferred_element_type=F32).astype(BF)
+            t = jnp.dot(ex_m[c, pl.ds(o, 256), :], sc, preferred_element_type=F32).astype(BF)
             out[pl.ds(o, 256), :] = t if first else out[pl.ds(o, 256), :] + t
+            if last:
+                pltpu.make_async_copy(out.at[pl.ds(o, 256), :], out_hbm.at[pl.ds(o, 256), :], loc.at[9]).start()
+
+        if last:
+            pltpu.make_async_copy(out, out_hbm, loc.at[9]).wait()
+
+    def ex(c):
+        slots = (lax.broadcasted_iota(jnp.int32, (128, CH), 1) + c * CH).astype(F32)
+        for a in range(12):
+            ex_m[c, pl.ds(a * 128, 128), :] = jnp.where(slots == scol[:, a:a + 1], 1.0, 0.0).astype(BF)
 
     barrier = pltpu.get_barrier_semaphore()
     for i, to in STAGES:
@@ -314,20 +349,21 @@
     pkm[...] = jnp.zeros_like(pkm)
 
     steps = (
-        (pick, 0), (own, 0, 1), (pick, 2), (own, 0, 0), (load,), (pick, 1), (w1,), (r, 0, 1, 1), (f, 0, 1, 0),
-        (r, 0, 1, 3), (r, 0, 0, 3), (f, 0, 0, 0), (r, 0, 0, 1), (own, 1, 0), (r, 0, 1, 2), (f, 0, 0, 1),
-        (f, 1, 0, 0), (w2,), (f, 0, 1, 1), (f, 0, 1, 3), (r, 1, 0, 1), (r, 0, 0, 2), (own, 1, 1), (gu, 0, 0),
-        (r, 1, 0, 3), (f, 1, 0, 1), (f, 0, 1, 2), (gu, 0, 3), (r, 1, 0, 2), (f, 1, 1, 0), (f, 0, 0, 2),
-        (gu, 0, 1), (r, 1, 1, 1), (own, 2, 0), (own, 2, 1), (f, 0, 0, 3), (f, 1, 0, 3), (gu, 1, 0),
-        (r, 1, 1, 3), (f, 1, 1, 1), (f, 1, 0, 2), (r, 2, 0, 1), (r, 2, 0, 3), (r, 2, 1, 1), (f, 2, 1, 0),
-        (r, 2, 1, 3), (f, 1, 1, 3), (gu, 0, 2), (act, 0), (gu, 1, 1), (r, 2, 0, 2), (f, 2, 1, 1),
-        (f, 2, 0, 1), (r, 1, 1, 2), (f, 2, 1, 3), (f, 2, 0, 3), (gu, 2, 0), (gu, 1, 3), (r, 2, 1, 2),
-        (f, 2, 0, 2), (f, 1, 1, 2), (gu, 2, 1), (f, 2, 1, 2), (rot, 0), (f, 2, 0, 0), (by, 0), (gu, 1, 2),
-        (act, 1), (gu, 2, 3), (gu, 2, 2), (act, 2), (bx, 0), (rot, 1), (by, 1), (bf, 0, 1), (bf, 0, -1),
-        (rot, 2), (pks_, 0), (by, 2), (bx, 1), (pkw, 0), (pks_, 1), (bx, 2), (bf, 1, 1), (bf, 1, -1),
-        (bf, 2, 1), (bf, 2, -1), (pkw, 1), (clip, 0), (d, 0, 2), (d, 0, -1), (d, 0, 0), (clip, 1), (d, 1, 2),
-        (d, 1, 0), (d, 1, 1), (d, 1, -1), (clip, 2), (d, 2, 2), (d, 2, 1), (s, 1, 1), (s, 1, -1), (d, 2, 0),
-        (d, 0, 1), (s, 0, 1), (s, 0, -1), (d, 2, -1), (s, 2, 1), (s, 2, -1), (fin, 1), (fin, 0), (fin, 2),
+        (head,), (pick, 0), (own, 0, 0), (w1,), (ex, 2), (ex, 0), (own, 0, 1), (load,), (ex, 1), (pick, 1),
+        (r, 0, 0, 3), (f, 0, 0, 0), (pick, 2), (r, 0, 1, 3), (r, 0, 1, 1), (f, 0, 0, 3), (r, 0, 1, 2),
+        (f, 0, 1, 0), (r, 0, 0, 2), (own, 1, 1), (own, 1, 0), (f, 0, 1, 3), (f, 0, 1, 1), (w2,), (f, 0, 0, 2),
+        (gu, 0, 0), (r, 1, 1, 3), (r, 1, 1, 1), (f, 1, 1, 0), (r, 1, 0, 1), (f, 1, 0, 0), (r, 1, 0, 3),
+        (f, 1, 1, 3), (f, 0, 1, 2), (r, 0, 0, 1), (f, 1, 0, 1), (r, 1, 1, 2), (f, 1, 1, 1), (f, 1, 0, 3),
+        (r, 1, 0, 2), (own, 2, 0), (own, 2, 1), (gu, 0, 1), (f, 0, 0, 1), (gu, 1, 0), (f, 1, 1, 2),
+        (gu, 0, 3), (r, 2, 0, 3), (f, 1, 0, 2), (gu, 1, 1), (gu, 1, 3), (r, 2, 0, 1), (f, 2, 0, 0),
+        (f, 2, 1, 0), (r, 2, 1, 1), (r, 2, 1, 3), (gu, 0, 2), (r, 2, 0, 2), (act, 0), (f, 2, 0, 3),
+        (f, 2, 0, 1), (gu, 2, 0), (f, 2, 1, 1), (gu, 1, 2), (r, 2, 1, 2), (f, 2, 1, 3), (act, 1),
+        (f, 2, 0, 2), (gu, 2, 1), (f, 2, 1, 2), (rot, 0), (gu, 2, 3), (by, 0), (gu, 2, 2), (act, 2), (rot, 1),
+        (by, 1), (bx, 0), (rot, 2), (pks_, 0), (by, 2), (bf, 0, 1), (bf, 0, -1), (bx, 1), (pkw, 0), (pks_, 1),
+        (bx, 2), (bf, 1, 1), (bf, 1, -1), (bf, 2, 1), (bf, 2, -1), (pkw, 1), (clip, 0), (d, 0, 2), (d, 0, -1),
+        (d, 0, 1), (clip, 1), (d, 1, 2), (clip, 2), (d, 2, 2), (s, 0, 1), (s, 0, -1), (d, 2, 1), (d, 1, 1),
+        (d, 1, -1), (s, 1, 1), (s, 1, -1), (s, 2, 1), (d, 2, -1), (s, 2, -1), (d, 1, 0), (d, 2, 0), (d, 0, 0),
+        (fin, 0), (fin, 1), (fin, 2),
     )
     for step, *args in steps:
         step(*args)
@@ -347,28 +383,15 @@
         wait_s(pkr.at[i, pl.ds(0, len(STAGES[i][0]))], pk_s.at[i])
 
 
-def hadamard(n):
-    i = jnp.arange(n, dtype=jnp.int32)
-    v = i[:, None] & i[None, :]
-    p = jnp.zeros_like(v)
-    for b in range(n.bit_length() - 1):
-        p = p ^ (v >> b & 1)
-    return (1 - 2 * p).astype(BF)
-
-
 def on_device(tokens, expert_ids, gate_probs, gate_weight, up_weight, down_weight):
-    hits = expert_ids == 0
-    routed = jnp.any(hits, axis=1)
-    share = jnp.sum(jnp.where(hits, gate_probs, 0.0), axis=1)
-    slot = jnp.where(routed, jnp.cumsum(routed.astype(jnp.int32)) - 1, -1)
     vm, anyspace = pl.BlockSpec(memory_space=pltpu.VMEM), pl.BlockSpec(memory_space=pl.ANY)
     V, DMA = pltpu.VMEM, pltpu.SemaphoreType.DMA
     out, peaks = pl.pallas_call(
         body,
         name="expert",
-        out_shape=(jax.ShapeDtypeStruct((TOK, SL), BF), jax.ShapeDtypeStruct((8, 128), F32)),
-        in_specs=[vm] * 5 + [anyspace] * 3,
-        out_specs=(vm, vm),
+        out_shape=(jax.ShapeDtypeStruct((TOK, SL), BF), jax.ShapeDtypeStruct((2,), F32)),
+        in_specs=[vm] * 2 + [anyspace] * 4,
+        out_specs=(anyspace, pl.BlockSpec(memory_space=pltpu.SMEM)),
         scratch_shapes=[
             V((16, CAP, SL), BF),
             V((4, D, 256), BF),
@@ -389,6 +412,12 @@
             V((3, 8, 128), F32),
             V((2, 15, 8, 128), F32),
             V((8, 128), F32),
+            V((2, TOK), F32),
+            V((128, 128), F32),
+            V((NCH, TOK, CH), BF),
+            V((TOK, SL), BF),
+            V((TOK, SL), BF),
+            V((128, 128), BF),
             DMA((NCH, 2, 15)), DMA((NCH, 2)),
             DMA((NCH,)), DMA((NCH,)),
             DMA((NCH, 3)), DMA((NCH,)),
@@ -397,12 +426,12 @@
             DMA((3,)), DMA((3,)),
             DMA((3, 3)), DMA((3,)),
             DMA((2,)), DMA((2,)),
-            DMA((8,)),
+            DMA((10,)),
         ],
         compiler_params=pltpu.CompilerParams(
             collective_id=0, has_side_effects=True, vmem_limit_bytes=66_000_000),
-    )(slot[None, :], share[None, :], slot[:, None], tokens, hadamard(128), gate_weight, up_weight, down_weight)
-    return out, peaks[:2, 0]
+    )(expert_ids.T, gate_probs.T, tokens, gate_weight, up_weight, down_weight)
+    return out, peaks
 
 
 def solution(mesh):

time: 126 us -> 119 us (0.944); the launches traced: 126 us -> 118 us
  other arithmetic: 4.31 us -> 0 us
  Pallas kernels: 116 us -> 113 us
  local copies, waits for them, and re-layouts: 4.79 us -> 3.53 us
    pallas_call x1, Pallas kernels: 116 us -> 113 us  [on_device(): pl.pallas_call(body, name='expert', out_shape=(jax.ShapeDtypeStruct((TOK,...]
    select_n x2 -> x0, other arithmetic: 1.76 us -> none  [on_device(): slot = jnp.where(routed, jnp.cumsum(routed.astype(jnp.int32)) - 1, -1)]
    slice x2 -> x0, local copies, waits for them, and re-layouts: 1.39 us -> none  [the longest x1 1.31 us: on_device(): return (out, peaks[:2, 0])]
where the time goes in v3:
time: 119 us; the launch traced here: 118 us
  Pallas kernels  113 us (95%)
  local copies, waits for them, and re-layouts  3.53 us (3%)
    pallas_call x1, Pallas kernels, on_device(): pl.pallas_call(body, name='expert', out_shape=(jax.ShapeDtypeStruct((TOK,...  113 us
    unnamed x2, local copies, waits for them, and re-layouts  3.53 us

profile of v3, /device:TPU:0, one launch (start us, length us, event | category | flops | bytes accessed | tf_op | source)
XLA Modules:
  0.0 117.5 jit_solution(16248799680518210669)
XLA Ops:
  0.6 113.4 %expert.1 = (bf16[1536,384]{1,0:T(8,128)(2,1)}, f32[2]{0:T(128)}) custom-call(s32[2,1536]{1,0:T(2,128)} %bitcast.2, f32[2,1536]{1,0:T(2,128)} %bitcast.3, bf16[1536,384]{1,0:T(8,128)(2,1)} %tok_hbm.1, bf16[6144,512]{1,0:T(8,128)(2,1)} %wg.1, bf16[6144,512]{1,0:T(8,128)(2,1)} %wu.1, bf16[512,6144]{1,0:T(8,128)(2,1)} %wd.1), custom_call_target="tpu_custom_call" | custom-call | tf_op jit(solution)/shard_map/expert/pallas_call | solution.py:389
  114.0 2.4 %copy.10 = bf16[1536,384]{1,0:T(8,128)(2,1)} copy(bf16[1536,384]{1,0:T(8,128)(2,1)} %get-tuple-element.4) | data formatting | bytes 2359296
  116.4 1.1 copy.11

commit v4 on v3

--- a/solution.py
+++ b/solution.py
@@ -86,9 +86,18 @@
     tok_copy = pltpu.make_async_copy(tok_hbm, tok, loc.at[8])
     tok_copy.start()
 
+    barrier = pltpu.get_barrier_semaphore()
+    for i, to in ((DEPTH, at_zc), (PLANE, at_uv)):
+        for t in i:
+            pl.semaphore_signal(barrier, inc=1, device_id=to(*t), device_id_type=MESH)
+
+    def here():
+        pl.semaphore_wait(barrier, len(PLANE) + len(DEPTH))
+
     me = v * 4 + u
 
     def head():
+        pkm[...] = jnp.zeros_like(pkm)
         i, j = (lax.broadcasted_iota(jnp.int32, (128, 128), a) for a in (0, 1))
         both, sign = i & j, jnp.zeros((128, 128), jnp.int32)
         for b in range(7):
@@ -341,28 +350,21 @@
         for a in range(12):
             ex_m[c, pl.ds(a * 128, 128), :] = jnp.where(slots == scol[:, a:a + 1], 1.0, 0.0).astype(BF)
 
-    barrier = pltpu.get_barrier_semaphore()
-    for i, to in STAGES:
-        for t in i:
-            pl.semaphore_signal(barrier, inc=1, device_id=to(*t), device_id_type=MESH)
-    pl.semaphore_wait(barrier, len(PLANE) + len(DEPTH))
-    pkm[...] = jnp.zeros_like(pkm)
-
     steps = (
-        (head,), (pick, 0), (own, 0, 0), (w1,), (ex, 2), (ex, 0), (own, 0, 1), (load,), (ex, 1), (pick, 1),
-        (r, 0, 0, 3), (f, 0, 0, 0), (pick, 2), (r, 0, 1, 3), (r, 0, 1, 1), (f, 0, 0, 3), (r, 0, 1, 2),
-        (f, 0, 1, 0), (r, 0, 0, 2), (own, 1, 1), (own, 1, 0), (f, 0, 1, 3), (f, 0, 1, 1), (w2,), (f, 0, 0, 2),
-        (gu, 0, 0), (r, 1, 1, 3), (r, 1, 1, 1), (f, 1, 1, 0), (r, 1, 0, 1), (f, 1, 0, 0), (r, 1, 0, 3),
-        (f, 1, 1, 3), (f, 0, 1, 2), (r, 0, 0, 1), (f, 1, 0, 1), (r, 1, 1, 2), (f, 1, 1, 1), (f, 1, 0, 3),
-        (r, 1, 0, 2), (own, 2, 0), (own, 2, 1), (gu, 0, 1), (f, 0, 0, 1), (gu, 1, 0), (f, 1, 1, 2),
-        (gu, 0, 3), (r, 2, 0, 3), (f, 1, 0, 2), (gu, 1, 1), (gu, 1, 3), (r, 2, 0, 1), (f, 2, 0, 0),
-        (f, 2, 1, 0), (r, 2, 1, 1), (r, 2, 1, 3), (gu, 0, 2), (r, 2, 0, 2), (act, 0), (f, 2, 0, 3),
-        (f, 2, 0, 1), (gu, 2, 0), (f, 2, 1, 1), (gu, 1, 2), (r, 2, 1, 2), (f, 2, 1, 3), (act, 1),
-        (f, 2, 0, 2), (gu, 2, 1), (f, 2, 1, 2), (rot, 0), (gu, 2, 3), (by, 0), (gu, 2, 2), (act, 2), (rot, 1),
-        (by, 1), (bx, 0), (rot, 2), (pks_, 0), (by, 2), (bf, 0, 1), (bf, 0, -1), (bx, 1), (pkw, 0), (pks_, 1),
-        (bx, 2), (bf, 1, 1), (bf, 1, -1), (bf, 2, 1), (bf, 2, -1), (pkw, 1), (clip, 0), (d, 0, 2), (d, 0, -1),
-        (d, 0, 1), (clip, 1), (d, 1, 2), (clip, 2), (d, 2, 2), (s, 0, 1), (s, 0, -1), (d, 2, 1), (d, 1, 1),
-        (d, 1, -1), (s, 1, 1), (s, 1, -1), (s, 2, 1), (d, 2, -1), (s, 2, -1), (d, 1, 0), (d, 2, 0), (d, 0, 0),
+        (head,), (pick, 0), (here,), (w1,), (own, 0, 0), (own, 0, 1), (load,), (pick, 2), (pick, 1),
+        (f, 0, 0, 0), (r, 0, 1, 3), (r, 0, 1, 1), (r, 0, 1, 2), (r, 0, 0, 3), (r, 0, 0, 1), (f, 0, 1, 0),
+        (f, 0, 1, 3), (w2,), (f, 0, 1, 1), (f, 0, 0, 3), (own, 1, 0), (f, 0, 1, 2), (f, 0, 0, 1), (own, 1, 1),
+        (r, 0, 0, 2), (f, 1, 0, 0), (gu, 0, 0), (r, 1, 1, 3), (r, 1, 0, 3), (r, 1, 0, 1), (f, 0, 0, 2),
+        (gu, 0, 3), (r, 1, 1, 1), (f, 1, 1, 0), (f, 1, 1, 3), (own, 2, 1), (gu, 0, 1), (r, 1, 1, 2),
+        (r, 1, 0, 2), (f, 1, 0, 3), (own, 2, 0), (f, 1, 0, 1), (gu, 1, 0), (gu, 0, 2), (f, 2, 1, 0), (ex, 1),
+        (r, 2, 1, 3), (ex, 0), (r, 2, 1, 1), (f, 1, 0, 2), (f, 1, 1, 1), (f, 1, 1, 2), (ex, 2), (r, 2, 0, 1),
+        (r, 2, 0, 3), (gu, 1, 3), (f, 2, 0, 0), (f, 2, 1, 3), (f, 2, 1, 1), (r, 2, 1, 2), (act, 0),
+        (gu, 1, 1), (f, 2, 0, 1), (gu, 1, 2), (f, 2, 0, 3), (r, 2, 0, 2), (gu, 2, 0), (f, 2, 1, 2),
+        (f, 2, 0, 2), (act, 1), (gu, 2, 3), (gu, 2, 1), (rot, 0), (by, 0), (gu, 2, 2), (act, 2), (rot, 1),
+        (by, 1), (bx, 0), (rot, 2), (by, 2), (pks_, 0), (bf, 0, -1), (bf, 0, 1), (bx, 1), (pkw, 0), (pks_, 1),
+        (bx, 2), (bf, 1, 1), (bf, 1, -1), (bf, 2, -1), (bf, 2, 1), (pkw, 1), (clip, 0), (d, 0, 2), (d, 0, -1),
+        (d, 0, 1), (clip, 1), (d, 1, 2), (clip, 2), (d, 2, 2), (s, 0, 1), (s, 0, -1), (d, 1, 1), (d, 2, 0),
+        (d, 1, -1), (s, 1, 1), (s, 1, -1), (d, 2, 1), (s, 2, 1), (d, 2, -1), (s, 2, -1), (d, 1, 0), (d, 0, 0),
         (fin, 0), (fin, 1), (fin, 2),
     )
     for step, *args in steps:

time: 119 us -> 117 us (0.983)
    pallas_call x1, Pallas kernels: 113 us -> 112 us  [on_device(): pl.pallas_call(body, name='expert', out_shape=(jax.ShapeDtypeStruct((TOK,...]
where the time goes in v4:
time: 117 us; the launch traced here: 116 us
  Pallas kernels  112 us (96%)
  local copies, waits for them, and re-layouts  3.53 us (3%)
    pallas_call x1, Pallas kernels, on_device(): pl.pallas_call(body, name='expert', out_shape=(jax.ShapeDtypeStruct((TOK,...  112 us
    unnamed x2, local copies, waits for them, and re-layouts  3.53 us

profile of v4, /device:TPU:0, one launch (start us, length us, event | category | flops | bytes accessed | tf_op | source)
XLA Modules:
  0.0 116.2 jit_solution(10977323979937221340)
XLA Ops:
  0.6 112.0 %expert.1 = (bf16[1536,384]{1,0:T(8,128)(2,1)}, f32[2]{0:T(128)}) custom-call(s32[2,1536]{1,0:T(2,128)} %bitcast.2, f32[2,1536]{1,0:T(2,128)} %bitcast.3, bf16[1536,384]{1,0:T(8,128)(2,1)} %tok_hbm.1, bf16[6144,512]{1,0:T(8,128)(2,1)} %wg.1, bf16[6144,512]{1,0:T(8,128)(2,1)} %wu.1, bf16[512,6144]{1,0:T(8,128)(2,1)} %wd.1), custom_call_target="tpu_custom_call" | custom-call | tf_op jit(solution)/shard_map/expert/pallas_call | solution.py:391
  112.7 2.4 %copy.10 = bf16[1536,384]{1,0:T(8,128)(2,1)} copy(bf16[1536,384]{1,0:T(8,128)(2,1)} %get-tuple-element.4) | data formatting | bytes 2359296
  115.1 1.1 copy.11

commit v5 on v4

--- a/solution.py
+++ b/solution.py
@@ -309,25 +309,27 @@
         elif k == 0:
             of[c] = t
         else:
-            pf[c, (k + 1) // 2] = t
+            side = (k + 1) // 2
+            free, kept = (hi, lo) if k == -1 else (lo, hi)
+            pf[c, side, kept, :] = t[:128] if k == -1 else t[128:]
+            s2[c, side, free, :] = (t[128:] if k == -1 else t[:128]).astype(BF)
+            send(s2.at[c, side, free, :], r2.at[c, side, free, :], t_s.at[c, 1], t_r.at[c, 4 + side], at_uv(0, k))
 
     def s(c, k):
         if k == -1:
             need(("t", c, 0), r1.at[c, lo, :], t_r.at[c, 0])
             s2[c, 0, lo, :] = (pf[c, 0, lo, :] + r1[c, lo, :].astype(F32)).astype(BF)
-            s2[c, 0, hi, :] = pf[c, 0, hi, :].astype(BF)
-            send(s2.at[c, 0], r2.at[c, 0], t_s.at[c, 1], t_r.at[c, 2], at_uv(0, -1))
+            send(s2.at[c, 0, lo, :], r2.at[c, 0, lo, :], t_s.at[c, 1], t_r.at[c, 2], at_uv(0, -1))
         else:
             need(("t", c, 1), r1.at[c, hi, :], t_r.at[c, 1])
-            s2[c, 1, lo, :] = pf[c, 1, lo, :].astype(BF)
             s2[c, 1, hi, :] = (pf[c, 1, hi, :] + r1[c, hi, :].astype(F32)).astype(BF)
-            send(s2.at[c, 1], r2.at[c, 1], t_s.at[c, 1], t_r.at[c, 3], at_uv(0, 1))
+            send(s2.at[c, 1, hi, :], r2.at[c, 1, hi, :], t_s.at[c, 1], t_r.at[c, 3], at_uv(0, 1))
 
     done = set()
 
     def fin(c):
-        need(("t", c, 2), r2.at[c, 0], t_r.at[c, 2])
-        need(("t", c, 3), r2.at[c, 1], t_r.at[c, 3])
+        for i, side, part in ((2, 0, lo), (4, 0, hi), (3, 1, hi), (5, 1, lo)):
+            need(("t", c, i), r2.at[c, side, part, :], t_r.at[c, i])
         tot = of[c] + r2[c, 0].astype(F32) + r2[c, 1].astype(F32)
         sc = (tot * shs[pl.ds(c * CH, CH), :]).astype(BF)
         first = not done
@@ -424,7 +426,7 @@
             DMA((NCH,)), DMA((NCH,)),
             DMA((NCH, 3)), DMA((NCH,)),
             DMA((NCH, 6)), DMA((NCH,)),
-            DMA((NCH, 4)), DMA((NCH, 2)),
+            DMA((NCH, 6)), DMA((NCH, 2)),
             DMA((3,)), DMA((3,)),
             DMA((3, 3)), DMA((3,)),
             DMA((2,)), DMA((2,)),

time: 117 us -> 117 us (level)
  no operation moved by 1% of the time
where the time goes in v5:
time: 117 us
  Pallas kernels  113 us (97%)
  local copies, waits for them, and re-layouts  3.53 us (3%)
    pallas_call x1, Pallas kernels, on_device(): pl.pallas_call(body, name='expert', out_shape=(jax.ShapeDtypeStruct((TOK,...  113 us
    unnamed x2, local copies, waits for them, and re-layouts  3.53 us

profile of v5, /device:TPU:0, one launch (start us, length us, event | category | flops | bytes accessed | tf_op | source)
XLA Modules:
  0.0 116.9 jit_solution(7875747532042161538)
XLA Ops:
  0.6 112.7 %expert.1 = (bf16[1536,384]{1,0:T(8,128)(2,1)}, f32[2]{0:T(128)}) custom-call(s32[2,1536]{1,0:T(2,128)} %bitcast.2, f32[2,1536]{1,0:T(2,128)} %bitcast.3, bf16[1536,384]{1,0:T(8,128)(2,1)} %tok_hbm.1, bf16[6144,512]{1,0:T(8,128)(2,1)} %wg.1, bf16[6144,512]{1,0:T(8,128)(2,1)} %wu.1, bf16[512,6144]{1,0:T(8,128)(2,1)} %wd.1), custom_call_target="tpu_custom_call" | custom-call | tf_op jit(solution)/shard_map/expert/pallas_call | solution.py:393
  113.4 2.4 %copy.10 = bf16[1536,384]{1,0:T(8,128)(2,1)} copy(bf16[1536,384]{1,0:T(8,128)(2,1)} %get-tuple-element.4) | data formatting | bytes 2359296
  115.8 1.1 copy.11
